TPU v7x, 32 devices: a whole 2x2x4 slice. The times are simulated.
32 devices in a mesh: seq: 4 (over y, core), user: 8 (over z, x).
Axes of the slice: x: 2, y: 2, z: 4, core: 2. Of those that a mesh axis runs over, the one named last changes fastest.
Arguments:
- history: bfloat16 [8, 2048, 256], P('user', 'seq'), may hold values from -6 to 6
- cotangent: bfloat16 [8, 2048, 256], P('user', 'seq'), may hold values from -6 to 6
- weights: bfloat16 [4, 3, 256, 256], replicated, may hold values from -0.21875 to 0.21875
- ln_gain: float32 [4, 256], replicated, may hold values from 0.1 to 1.9
- conv_bias: float32 [4, 256], replicated, may hold values from -3 to 3
- pooled_grad: bfloat16 [8, 64, 128], P('user', 'seq'), may hold values from -6 to 6
- table_owner: int32 [64], P('seq'), may hold values from 0 to 7, as said below
- row_ids: int32 [8, 64], P('user', 'seq'), may hold values from 0 to 999999
Outputs:
- d_history: bfloat16 [8, 2048, 256], P('user', 'seq')
- grad_weights: float32 [4, 3, 256, 256], replicated
- grad_gain: float32 [4, 256], replicated
- grad_bias: float32 [4, 256], replicated
- table_grad: float32 [64, 8, 128], P(('seq', 'user'))
Inputs may be any that keep to these rules, and one draw needn't show every extreme that they name: `table_owner`: within each block of 16 consecutive tables, every user index owns exactly 2 tables.
All inputs are finite; a program needn't handle non-finite values.
Results may differ from a plain program's by a relative error of at most 0.0095.
Values may be sent and summed in bfloat16 or wider, within the bound.
A program may use at most 64 MiB of HBM per device.

v0:
```python
import math
import jax
import jax.numpy as jnp
from jax import lax
from jax.sharding import PartitionSpec as P

TAPS = 3
LAYERS = 4
epsilon = 1e-05


def passed_along(block, axis, distance):
    devices = range(lax.axis_size(axis))
    route = [(i - distance, i) for i in devices if i - distance in devices]
    return lax.ppermute(block, axis, route)


def gelu_tanh(values):
    return jax.nn.gelu(values, approximate=True)


def gelu_slope(values, upstream):
    return jax.vjp(gelu_tanh, values)[1](upstream)[0]


def normalize(resid_field):
    center = resid_field - jnp.mean(resid_field, -1, keepdims=True)
    inverse = lax.rsqrt(jnp.mean(center * center, -1, keepdims=True) + epsilon)
    return (center * inverse, inverse)


def dilated(padded, kernel, shift_bias, dilation):
    user_count, total_len, channels = padded.shape
    out_len = total_len - (TAPS - 1) * dilation
    result = jnp.zeros((user_count * out_len, kernel.shape[2]), jnp.float32) + shift_bias
    for tap_index in range(TAPS):
        offset = (TAPS - 1 - tap_index) * dilation
        window = padded[:, offset : offset + out_len].reshape(user_count * out_len, channels)
        result = result + jnp.dot(window, kernel[tap_index], preferred_element_type=jnp.float32)
    return result.reshape(user_count, out_len, kernel.shape[2])


def coalesce(pieces):
    got_rows, got_ids = pieces
    per_owner = got_rows.shape[2]
    flat_rows = got_rows.reshape(got_rows.shape[0], per_owner, got_rows.shape[3])
    key_grid = got_ids.reshape(got_ids.shape[0], per_owner).T
    matches = (key_grid[:, :, None] == key_grid[:, None, :]).astype(jnp.bfloat16)
    return jnp.einsum("tuv,vte->tue", matches, flat_rows, preferred_element_type=jnp.float32)


def body(history, cotangent, weights, ln_gain, conv_bias, pooled_grad, table_owner, row_ids):
    user_count, length, channels = history.shape
    row_count = user_count * length
    stored = []
    resid_field = history.astype(jnp.float32)
    for layer_num in range(LAYERS):
        dilation = 2**layer_num
        lookback = (TAPS - 1) * dilation
        normed, inverse = normalize(resid_field)
        hidden = gelu_tanh(normed * ln_gain[layer_num]).astype(jnp.bfloat16)
        border = passed_along(hidden[:, length - lookback :], "seq", 1)
        padded = jnp.concatenate([border, hidden], 1)
        stored.append((resid_field, padded))
        resid_field = resid_field + dilated(
            padded, weights[layer_num], conv_bias[layer_num], dilation
        )
    grad_flow = cotangent.astype(jnp.float32)
    weight_terms = [None] * LAYERS
    gain_terms = [None] * LAYERS
    bias_terms = [None] * LAYERS
    for layer_num in reversed(range(LAYERS)):
        dilation = 2**layer_num
        lookback = (TAPS - 1) * dilation
        field_in, padded = stored[layer_num]
        flow_half = grad_flow.astype(jnp.bfloat16)
        flow_flat = flow_half.reshape(row_count, channels)
        bias_terms[layer_num] = jnp.sum(grad_flow, (0, 1))
        tap_terms = []
        for tap_index in range(TAPS):
            offset = lookback - tap_index * dilation
            window = padded[:, offset : offset + length].reshape(row_count, channels)
            tap_terms.append(
                lax.dot_general(
                    window, flow_flat, (((0,), (0,)), ((), ())), preferred_element_type=jnp.float32
                )
            )
        weight_terms[layer_num] = jnp.stack(tap_terms)
        future = passed_along(flow_half[:, :lookback], "seq", -1)
        extended = jnp.concatenate([flow_half, future], 1)
        backward = jnp.zeros((row_count, channels), jnp.float32)
        for tap_index in range(TAPS):
            offset = tap_index * dilation
            window = extended[:, offset : offset + length].reshape(row_count, channels)
            backward = backward + lax.dot_general(
                window,
                weights[layer_num, tap_index],
                (((1,), (1,)), ((), ())),
                preferred_element_type=jnp.float32,
            )
        normed, inverse = normalize(field_in)
        slopes = gelu_slope(
            normed * ln_gain[layer_num], backward.reshape(user_count, length, channels)
        )
        gain_terms[layer_num] = jnp.sum(slopes * normed, (0, 1))
        scaled = slopes * ln_gain[layer_num]
        grad_flow = grad_flow + inverse * (
            scaled
            - jnp.mean(scaled, -1, keepdims=True)
            - normed * jnp.mean(scaled * normed, -1, keepdims=True)
        )
    weight_local = jnp.stack(weight_terms)
    gain_local = jnp.stack(gain_terms)
    bias_local = jnp.stack(bias_terms)
    weight_total, gain_total, bias_total = lax.psum(
        (weight_local, gain_local, bias_local), ("seq", "user")
    )
    factor = 1.0 / math.sqrt(user_count * lax.axis_size("user") * length * lax.axis_size("seq"))
    listing = jnp.argsort(table_owner, stable=True)
    per_owner = listing.shape[0] // lax.axis_size("user")
    send_rows = jnp.take(pooled_grad, listing, axis=1).reshape(
        user_count, lax.axis_size("user"), per_owner, pooled_grad.shape[2]
    )
    send_ids = jnp.take(row_ids, listing, axis=1).reshape(
        user_count, lax.axis_size("user"), per_owner
    )
    table_grad = coalesce(
        (
            lax.all_to_all(send_rows, "user", split_axis=1, concat_axis=0, tiled=True),
            lax.all_to_all(send_ids, "user", split_axis=1, concat_axis=0, tiled=True),
        )
    )
    return (
        grad_flow.astype(jnp.bfloat16),
        weight_total * factor,
        gain_total * factor,
        bias_total * factor,
        table_grad,
    )


def solution(mesh):
    in_specs = (
        P("user", "seq", None),
        P("user", "seq", None),
        P(),
        P(),
        P(),
        P("user", "seq", None),
        P("seq"),
        P("user", "seq"),
    )
    out_specs = (P("user", "seq", None), P(), P(), P(), P(("seq", "user"), None, None))
    return jax.shard_map(body, mesh=mesh, in_specs=in_specs, out_specs=out_specs, check_vma=False)
```

profile of v0, /device:TPU:0, one launch (start us, length us, event | category | flops | bytes accessed | tf_op | source)
XLA Modules:
  0.0 236.2 jit_solution(5344520800691517173)
XLA Ops:
  7.2 0.8 fusion.190
  8.0 1.1 convert_reduce_fusion
  9.2 1.2 fusion.30
  10.3 1.3 fusion.21
  11.6 2.4 %collective-permute-start = (bf16[1,2,256]{2,1,0:T(2,128)(2,1)S(1)}, bf16[1,2,256]{2,1,0:T(2,128)(2,1)S(1)}, u32[]{:S(2)}, u32[]{:S(2)}) collective-permute-start(bf16[1,2,256]{2,1,0:T(2,128)(2,1)S(1)} %slice.220), channel_id=1, source_target_pairs={{0,8},{8,16},{16,24},{1,9},{9,17},{17,25},{2,10},{10,18},{18,26},{... | collective-permute-start | bytes 3080 | tf_op jit(solution)/shard_map/ppermute | solution.py:15
  14.0 0.7 slice.198
  14.7 1.3 collective-permute-start.3
  16.0 1.9 sort.17
  17.9 1.3 gather_fusion
  19.3 0.7 reshape.430
  19.9 6.6 %all-to-all-start = ((s32[1,8,2]{2,0,1:T(1,128)}), s32[1,8,2]{2,0,1:T(1,128)S(1)}, u32[]{:S(2)}, u32[]{:S(2)}) async-start(s32[1,8,2]{2,0,1:T(1,128)} %bitcast.75), calls=%async_computation | async-start | bytes 8192 | tf_op jit(solution)/shard_map/all_to_all | solution.py:130
  26.6 1.2 fusion.104
  27.8 1.2 convolution_add_fusion.16
  29.6 0.7 fusion.162
  30.3 0.7 constant_dynamic-update-slice_fusion.1
  31.0 2.0 all-to-all-done
  33.0 4.0 %all-to-all-start.1 = ((bf16[1,8,2,128]{3,2,0,1:T(2,128)(2,1)}), bf16[1,8,2,128]{3,2,0,1:T(2,128)(2,1)S(1)}, u32[]{:S(2)}, u32[]{:S(2)}) async-start(bf16[1,8,2,128]{3,2,0,1:T(2,128)(2,1)} %fusion.162), calls=%async_computation.1 | async-start | bytes 8192 | tf_op jit(solution)/shard_map/all_to_all | solution.py:129
  37.2 1.1 convolution_add_fusion.15
  38.3 1.3 fusion.192
  40.1 3.5 %collective-permute-start.1 = (bf16[1,4,256]{2,1,0:T(4,128)(2,1)S(1)}, bf16[1,4,256]{2,1,0:T(4,128)(2,1)S(1)}, u32[]{:S(2)}, u32[]{:S(2)}) collective-permute-start(bf16[1,4,256]{2,1,0:T(4,128)(2,1)S(1)} %slice.223), channel_id=1, source_target_pairs={{0,8},{8,16},{16,24},{1,9},{9,17},{17,25},{2,10},{10,18},{18,26},{... | collective-permute-start | bytes 6152 | tf_op jit(solution)/shard_map/ppermute | solution.py:15
  43.7 1.1 convolution_add_fusion.13
  44.8 1.1 convolution_add_fusion.12
  46.0 1.3 fusion.193
  47.8 4.5 %collective-permute-start.2 = (bf16[1,8,256]{2,1,0:T(8,128)(2,1)S(1)}, bf16[1,8,256]{2,1,0:T(8,128)(2,1)S(1)}, u32[]{:S(2)}, u32[]{:S(2)}) collective-permute-start(bf16[1,8,256]{2,1,0:T(8,128)(2,1)S(1)} %slice.226), channel_id=1, source_target_pairs={{0,8},{8,16},{16,24},{1,9},{9,17},{17,25},{2,10},{10,18},{18,26},{... | collective-permute-start | bytes 12296 | tf_op jit(solution)/shard_map/ppermute | solution.py:15
  52.3 1.1 convolution_add_fusion.10
  53.4 1.1 convolution_add_fusion.9
  54.6 1.2 fusion.194
  56.1 0.8 fusion.160
  56.9 0.6 constant_dynamic-update-slice_fusion
  57.5 1.2 convolution_add_fusion.7
  58.8 1.8 multiply_reduce_fusion
  61.0 0.9 copy-done.3
  62.8 1.3 collective-permute-start.4
  64.1 4.3 %collective-permute-start.7 = (bf16[1,16,256]{2,1,0:T(8,128)(2,1)S(1)}, bf16[1,16,256]{2,1,0:T(8,128)(2,1)S(1)}, u32[]{:S(2)}, u32[]{:S(2)}) collective-permute-start(bf16[1,16,256]{2,1,0:T(8,128)(2,1)S(1)} %slice.240), channel_id=1, source_target_pairs={{0,8},{8,16},{16,24},{1,9},{9,17},{17,25},{2,10},{10,18},{18,26},{... | collective-permute-start | bytes 24584 | tf_op jit(solution)/shard_map/ppermute | solution.py:15
  69.3 0.8 multiply_reduce_fusion.1
  71.1 1.3 collective-permute-start.5
  73.0 2.5 %collective-permute-done.5 = bf16[1,4,256]{2,1,0:T(4,128)(2,1)S(1)} collective-permute-done((bf16[1,4,256]{2,1,0:T(4,128)(2,1)S(1)}, bf16[1,4,256]{2,1,0:T(4,128)(2,1)S(1)}, u32[]{:S(2)}, u32[]{:S(2)}) %collective-permute-start.5) | collective-permute-done | bytes 2080 | tf_op jit(solution)/shard_map/ppermute | solution.py:15
  75.7 0.8 multiply_reduce_fusion.2
  77.5 1.5 collective-permute-start.6
  80.2 2.1 pad_maximum_fusion
  82.4 1.2 convolution_add_fusion.1
  83.6 1.7 fusion.29
  85.3 44.3 %all-reduce = (f32[4,256]{1,0:T(4,128)S(1)}, f32[4,256]{1,0:T(4,128)S(1)}) all-reduce(f32[4,256]{1,0:T(4,128)S(1)} %pad_maximum_fusion.8, f32[4,256]{1,0:T(4,128)S(1)} %pad_maximum_fusion.9), channel_id=1, replica_groups=mesh['seq'=4,'user'=8] {'seq','user'}, use_global_device_ids=true, to_apply=%region_21.0 | all-reduce | flops 2048 | bytes 16384 | tf_op jit(solution)/shard_map/psum | solution.py:115
  129.6 0.6 broadcast_multiply_fusion.2
  130.2 0.6 broadcast_multiply_fusion.1
  130.8 1.0 fusion.28
  131.8 93.8 %all-reduce.3.cloned.1.call-done = f32[4,3,256,256]{3,2,1,0:T(8,128)} async-done(((f32[4,3,256,256]{3,2,1,0:T(8,128)}), f32[4,3,256,256]{3,2,1,0:T(8,128)}) %all-reduce.3.cloned.1.call-update) | async-done | bytes 3145744 | tf_op jit(solution)/shard_map/psum | solution.py:115
  225.6 3.8 %broadcast_multiply_fusion = f32[4,3,256,256]{3,2,1,0:T(8,128)} fusion(f32[4,3,256,256]{3,2,1,0:T(8,128)} %all-reduce.3.cloned.1.call-done), kind=kLoop, calls=%fused_computation.3 | loop fusion | flops 786432 | bytes 6291456 | tf_op jit(solution)/shard_map/mul | solution.py:135
  (83 shorter events, 8.4 us)
Async XLA Ops:
  7.2 21.8 %copy-start = (bf16[1,16,128]{2,1,0:T(8,128)(2,1)S(1)}, bf16[1,16,128]{2,1,0:T(8,128)(2,1)}, u32[]{:S(2)}) copy-start(bf16[1,16,128]{2,1,0:T(8,128)(2,1)} %param.13) | copy-start | bytes 12292
  7.2 19.4 %copy-start.2 = (bf16[1,512,256]{2,1,0:T(8,128)(2,1)S(1)}, bf16[1,512,256]{2,1,0:T(8,128)(2,1)}, u32[]{:S(2)}) copy-start(bf16[1,512,256]{2,1,0:T(8,128)(2,1)} %param.9) | copy-start | bytes 786436
  7.2 19.4 %copy-start.4 = (f32[4,256]{1,0:T(4,128)S(1)}, f32[4,256]{1,0:T(4,128)}, u32[]{:S(2)}) copy-start(f32[4,256]{1,0:T(4,128)} %param.12) | copy-start | bytes 12292
  11.6 25.5 %collective-permute-start = (bf16[1,2,256]{2,1,0:T(2,128)(2,1)S(1)}, bf16[1,2,256]{2,1,0:T(2,128)(2,1)S(1)}, u32[]{:S(2)}, u32[]{:S(2)}) collective-permute-start(bf16[1,2,256]{2,1,0:T(2,128)(2,1)S(1)} %slice.220), channel_id=1, source_target_pairs={{0,8},{8,16},{16,24},{1,9},{9,17},{17,25},{2,10},{10,18},{18,26},{... | collective-permute-start | bytes 3080 | tf_op jit(solution)/shard_map/ppermute | solution.py:15
  14.7 42.2 %collective-permute-start.3 = (bf16[1,16,256]{2,1,0:T(8,128)(2,1)S(1)}, bf16[1,16,256]{2,1,0:T(8,128)(2,1)S(1)}, u32[]{:S(2)}, u32[]{:S(2)}) collective-permute-start(bf16[1,16,256]{2,1,0:T(8,128)(2,1)S(1)} %slice.198), channel_id=1, source_target_pairs={{8,0},{16,8},{24,16},{9,1},{17,9},{25,17},{10,2},{18,10},{26,18},{... | collective-permute-start | bytes 24584 | tf_op jit(solution)/shard_map/ppermute | solution.py:15
  19.9 13.0 %all-to-all-start = ((s32[1,8,2]{2,0,1:T(1,128)}), s32[1,8,2]{2,0,1:T(1,128)S(1)}, u32[]{:S(2)}, u32[]{:S(2)}) async-start(s32[1,8,2]{2,0,1:T(1,128)} %bitcast.75), calls=%async_computation | async-start | bytes 8192 | tf_op jit(solution)/shard_map/all_to_all | solution.py:130
  27.8 10.5 %copy-start.1 = (bf16[1,512,256]{2,1,0:T(8,128)(2,1)S(1)}, bf16[1,512,256]{2,1,0:T(8,128)(2,1)}, u32[]{:S(2)}) copy-start(bf16[1,512,256]{2,1,0:T(8,128)(2,1)} %param.8) | copy-start | bytes 786436
  33.0 23.1 %all-to-all-start.1 = ((bf16[1,8,2,128]{3,2,0,1:T(2,128)(2,1)}), bf16[1,8,2,128]{3,2,0,1:T(2,128)(2,1)S(1)}, u32[]{:S(2)}, u32[]{:S(2)}) async-start(bf16[1,8,2,128]{3,2,0,1:T(2,128)(2,1)} %fusion.162), calls=%async_computation.1 | async-start | bytes 8192 | tf_op jit(solution)/shard_map/all_to_all | solution.py:129
  37.0 188.6 %all-reduce.3.cloned.1.call-start = ((), (), s32[]{:S(2)}) async-start(), calls=%async_computation.2 | async-start | bytes 6291456 | tf_op jit(solution)/shard_map/psum | solution.py:115
  40.1 4.6 %collective-permute-start.1 = (bf16[1,4,256]{2,1,0:T(4,128)(2,1)S(1)}, bf16[1,4,256]{2,1,0:T(4,128)(2,1)S(1)}, u32[]{:S(2)}, u32[]{:S(2)}) collective-permute-start(bf16[1,4,256]{2,1,0:T(4,128)(2,1)S(1)} %slice.223), channel_id=1, source_target_pairs={{0,8},{8,16},{16,24},{1,9},{9,17},{17,25},{2,10},{10,18},{18,26},{... | collective-permute-start | bytes 6152 | tf_op jit(solution)/shard_map/ppermute | solution.py:15
  47.8 5.6 %collective-permute-start.2 = (bf16[1,8,256]{2,1,0:T(8,128)(2,1)S(1)}, bf16[1,8,256]{2,1,0:T(8,128)(2,1)S(1)}, u32[]{:S(2)}, u32[]{:S(2)}) collective-permute-start(bf16[1,8,256]{2,1,0:T(8,128)(2,1)S(1)} %slice.226), channel_id=1, source_target_pairs={{0,8},{8,16},{16,24},{1,9},{9,17},{17,25},{2,10},{10,18},{18,26},{... | collective-permute-start | bytes 12296 | tf_op jit(solution)/shard_map/ppermute | solution.py:15
  60.5 1.4 copy-start.3
  62.8 6.3 %collective-permute-start.4 = (bf16[1,8,256]{2,1,0:T(8,128)(2,1)S(1)}, bf16[1,8,256]{2,1,0:T(8,128)(2,1)S(1)}, u32[]{:S(2)}, u32[]{:S(2)}) collective-permute-start(bf16[1,8,256]{2,1,0:T(8,128)(2,1)S(1)} %slice.231), channel_id=1, source_target_pairs={{8,0},{16,8},{24,16},{9,1},{17,9},{25,17},{10,2},{18,10},{26,18},{... | collective-permute-start | bytes 12296 | tf_op jit(solution)/shard_map/ppermute | solution.py:15
  64.1 15.5 %collective-permute-start.7 = (bf16[1,16,256]{2,1,0:T(8,128)(2,1)S(1)}, bf16[1,16,256]{2,1,0:T(8,128)(2,1)S(1)}, u32[]{:S(2)}, u32[]{:S(2)}) collective-permute-start(bf16[1,16,256]{2,1,0:T(8,128)(2,1)S(1)} %slice.240), channel_id=1, source_target_pairs={{0,8},{8,16},{16,24},{1,9},{9,17},{17,25},{2,10},{10,18},{18,26},{... | collective-permute-start | bytes 24584 | tf_op jit(solution)/shard_map/ppermute | solution.py:15
  71.1 4.4 %collective-permute-start.5 = (bf16[1,4,256]{2,1,0:T(4,128)(2,1)S(1)}, bf16[1,4,256]{2,1,0:T(4,128)(2,1)S(1)}, u32[]{:S(2)}, u32[]{:S(2)}) collective-permute-start(bf16[1,4,256]{2,1,0:T(4,128)(2,1)S(1)} %slice.234), channel_id=1, source_target_pairs={{8,0},{16,8},{24,16},{9,1},{17,9},{25,17},{10,2},{18,10},{26,18},{... | collective-permute-start | bytes 6152 | tf_op jit(solution)/shard_map/ppermute | solution.py:15
  77.5 4.9 %collective-permute-start.6 = (bf16[1,2,256]{2,1,0:T(2,128)(2,1)S(1)}, bf16[1,2,256]{2,1,0:T(2,128)(2,1)S(1)}, u32[]{:S(2)}, u32[]{:S(2)}) collective-permute-start(bf16[1,2,256]{2,1,0:T(2,128)(2,1)S(1)} %slice.237), channel_id=1, source_target_pairs={{8,0},{16,8},{24,16},{9,1},{17,9},{25,17},{10,2},{18,10},{26,18},{... | collective-permute-start | bytes 3080 | tf_op jit(solution)/shard_map/ppermute | solution.py:15
Sparse Core Ops, SparseCore 0:
  82.4 143.1 all-reduce.2
where the time goes:
time: 237 us; the launch traced here: 236 us
  waiting for transfers between devices  98.4 us (42%)
  blocking collectives  44.3 us (19%)
  starting transfers between devices  30.8 us (13%)
  matrix products  24.5 us (10%)
  other arithmetic  17.1 us (7%)
  between operations  14.6 us (6%)
  local copies, waits for them, and re-layouts  6.56 us (3%)
    psum x1, waiting for transfers between devices, body(): lax.psum((weight_local, gain_local, bias_local), ('seq', 'user'))  93.8 us
    psum x1, blocking collectives, body(): lax.psum((weight_local, gain_local, bias_local), ('seq', 'user'))  44.3 us
    ppermute x8, starting transfers between devices, passed_along(): return lax.ppermute(block, axis, route)  20.1 us
    dot_general x9, matrix products, dilated(): jnp.dot(window, kernel[tap_index], preferred_element_type=jnp.float32)  10.6 us
    dot_general x12, matrix products, body(): lax.dot_general(window, weights[layer_num, tap_index], (((1,), (1,)), (()...  9.9 us
    all_to_all x1, starting transfers between devices, body(): lax.all_to_all(send_ids, 'user', split_axis=1, concat_axis=0, tiled=True)  6.62 us
  transfers between devices with their start and end apart: 11, of which 4 were waited for; matrix products, arithmetic and copies ran while one was open for 14% of the time, Pallas kernels for 0%

commit v1 on v0

--- a/solution.py
+++ b/solution.py
@@ -113,7 +113,7 @@
     gain_local = jnp.stack(gain_terms)
     bias_local = jnp.stack(bias_terms)
     weight_total, gain_total, bias_total = lax.psum(
-        (weight_local, gain_local, bias_local), ("seq", "user")
+        lax.psum((weight_local, gain_local, bias_local), "seq"), "user"
     )
     factor = 1.0 / math.sqrt(user_count * lax.axis_size("user") * length * lax.axis_size("seq"))
     listing = jnp.argsort(table_owner, stable=True)

time: 237 us -> 268 us (1.13)
  waiting for transfers between devices: 98.4 us -> 161 us
  blocking collectives: 44.3 us -> 26.8 us
  matrix products: 24.5 us -> 12.6 us
    psum x1 -> x2, waiting for transfers between devices: 93.8 us -> 144 us  [the longest x1 74.9 us: body(): lax.psum(lax.psum((weight_local, gain_local, bias_local), 'seq'), 'user')]
    psum x1 -> x2, blocking collectives: 44.3 us -> 26.8 us  [the longest x1 19.4 us: body(): lax.psum(lax.psum((weight_local, gain_local, bias_local), 'seq'), 'user')]
    dot_general x9, matrix products: 10.6 us -> 2.42 us  [dilated(): jnp.dot(window, kernel[tap_index], preferred_element_type=jnp.float32)]
    all_to_all x1, waiting for transfers between devices: 0.01 us -> 6.53 us  [body(): lax.all_to_all(send_rows, 'user', split_axis=1, concat_axis=0, tiled=True)]
    dot_general x12, matrix products: 9.9 us -> 6.2 us  [body(): lax.dot_general(window, weights[layer_num, tap_index], (((1,), (1,)), (()...]
    all_to_all x1, waiting for transfers between devices: 1.96 us -> 5.2 us  [body(): lax.all_to_all(send_ids, 'user', split_axis=1, concat_axis=0, tiled=True)]
    ppermute x8, waiting for transfers between devices: 2.64 us -> 5.55 us  [passed_along(): return lax.ppermute(block, axis, route)]
  transfers between devices with their start and end apart: 11 -> 12, of which waited for: 4 -> 8; matrix products, arithmetic and copies ran while one was open for 14% -> 8% of each run, Pallas kernels for 0% -> 0%
where the time goes in v1:
time: 268 us
  waiting for transfers between devices  161 us (60%)
  starting transfers between devices  29.9 us (11%)
  blocking collectives  26.8 us (10%)
  other arithmetic  16.5 us (6%)
  between operations  14.7 us (5%)
  matrix products  12.6 us (5%)
  local copies, waits for them, and re-layouts  6.12 us (2%)
    psum x1, waiting for transfers between devices, body(): lax.psum(lax.psum((weight_local, gain_local, bias_local), 'seq'), 'user')  74.9 us
    psum x1, waiting for transfers between devices, body(): lax.psum((weight_local, gain_local, bias_local), 'seq')  69 us
    ppermute x8, starting transfers between devices, passed_along(): return lax.ppermute(block, axis, route)  21 us
    psum x1, blocking collectives, body(): lax.psum(lax.psum((weight_local, gain_local, bias_local), 'seq'), 'user')  19.4 us
    psum x1, blocking collectives, body(): lax.psum((weight_local, gain_local, bias_local), 'seq')  7.43 us
    all_to_all x1, waiting for transfers between devices, body(): lax.all_to_all(send_rows, 'user', split_axis=1, concat_axis=0, tiled=True)  6.53 us
    dot_general x12, matrix products, body(): lax.dot_general(window, weights[layer_num, tap_index], (((1,), (1,)), (()...  6.2 us
    ppermute x8, waiting for transfers between devices, passed_along(): return lax.ppermute(block, axis, route)  5.55 us
  transfers between devices with their start and end apart: 12, of which 8 were waited for; matrix products, arithmetic and copies ran while one was open for 8% of the time, Pallas kernels for 0%

profile of v1, /device:TPU:0, one launch (start us, length us, event | category | flops | bytes accessed | tf_op | source)
XLA Modules:
  0.0 267.7 jit_solution(2381350296428647668)
XLA Ops:
  7.2 0.9 fusion.190
  8.1 1.1 convert_reduce_fusion
  9.2 1.2 fusion.30
  10.4 1.3 fusion.21
  11.7 2.4 collective-permute-start
  14.1 0.7 slice.198
  14.8 1.3 collective-permute-start.3
  16.1 0.8 fusion.191
  16.9 1.2 fusion.104
  18.7 0.4 copy-done.2
  20.0 5.2 %collective-permute-start.1 = (bf16[1,4,256]{2,1,0:T(4,128)(2,1)S(1)}, bf16[1,4,256]{2,1,0:T(4,128)(2,1)S(1)}, u32[]{:S(2)}, u32[]{:S(2)}) collective-permute-start(bf16[1,4,256]{2,1,0:T(4,128)(2,1)S(1)} %slice.223), channel_id=1, source_target_pairs={{0,8},{8,16},{16,24},{1,9},{9,17},{17,25},{2,10},{10,18},{18,26},{... | collective-permute-start | bytes 6152 | tf_op jit(solution)/shard_map/ppermute | solution.py:15
  25.4 0.6 collective-permute-done.1
  27.2 3.5 %collective-permute-start.2 = (bf16[1,8,256]{2,1,0:T(8,128)(2,1)S(1)}, bf16[1,8,256]{2,1,0:T(8,128)(2,1)S(1)}, u32[]{:S(2)}, u32[]{:S(2)}) collective-permute-start(bf16[1,8,256]{2,1,0:T(8,128)(2,1)S(1)} %slice.226), channel_id=1, source_target_pairs={{0,8},{8,16},{16,24},{1,9},{9,17},{17,25},{2,10},{10,18},{18,26},{... | collective-permute-start | bytes 12296 | tf_op jit(solution)/shard_map/ppermute | solution.py:15
  31.0 0.6 collective-permute-done.2
  32.7 0.8 multiply_reduce_fusion
  33.4 0.5 fusion.189
  34.8 1.3 collective-permute-start.4
  36.1 4.7 %collective-permute-start.7 = (bf16[1,16,256]{2,1,0:T(8,128)(2,1)S(1)}, bf16[1,16,256]{2,1,0:T(8,128)(2,1)S(1)}, u32[]{:S(2)}, u32[]{:S(2)}) collective-permute-start(bf16[1,16,256]{2,1,0:T(8,128)(2,1)S(1)} %slice.240), channel_id=1, source_target_pairs={{0,8},{8,16},{16,24},{1,9},{9,17},{17,25},{2,10},{10,18},{18,26},{... | collective-permute-start | bytes 24584 | tf_op jit(solution)/shard_map/ppermute | solution.py:15
  41.7 0.8 multiply_reduce_fusion.1
  42.5 0.4 fusion.188
  43.5 1.3 collective-permute-start.5
  45.4 2.9 %collective-permute-done.5 = bf16[1,4,256]{2,1,0:T(4,128)(2,1)S(1)} collective-permute-done((bf16[1,4,256]{2,1,0:T(4,128)(2,1)S(1)}, bf16[1,4,256]{2,1,0:T(4,128)(2,1)S(1)}, u32[]{:S(2)}, u32[]{:S(2)}) %collective-permute-start.5) | collective-permute-done | bytes 2080 | tf_op jit(solution)/shard_map/ppermute | solution.py:15
  48.6 0.8 multiply_reduce_fusion.2
  49.4 0.4 fusion.187
  51.3 2.1 pad_maximum_fusion
  53.4 0.6 copy-done.5
  54.0 1.2 sort.17
  55.2 69.0 %all-reduce.5.cloned.1.call-done = f32[4,3,256,256]{3,2,1,0:T(8,128)} async-done(((f32[4,3,256,256]{3,2,1,0:T(8,128)}), f32[4,3,256,256]{3,2,1,0:T(8,128)}) %all-reduce.5.cloned.1.call-update) | async-done | bytes 3145744 | tf_op jit(solution)/shard_map/psum | solution.py:116
  124.3 0.6 copy-done.1
  124.9 0.7 gather_fusion
  125.5 0.7 reshape.430
  126.2 5.5 %all-to-all-start = ((s32[1,8,2]{2,0,1:T(1,128)}), s32[1,8,2]{2,0,1:T(1,128)S(1)}, u32[]{:S(2)}, u32[]{:S(2)}) async-start(s32[1,8,2]{2,0,1:T(1,128)} %bitcast.75), calls=%async_computation | async-start | bytes 8192 | tf_op jit(solution)/shard_map/all_to_all | solution.py:130
  131.7 0.6 gather_fusion.1
  132.4 0.7 fusion.162
  133.1 5.2 %all-to-all-done = s32[1,8,2]{2,0,1:T(1,128)S(1)} async-done(((s32[1,8,2]{2,0,1:T(1,128)}), s32[1,8,2]{2,0,1:T(1,128)S(1)}, u32[]{:S(2)}, u32[]{:S(2)}) %all-to-all-start) | async-done | bytes 96 | tf_op jit(solution)/shard_map/all_to_all | solution.py:130
  138.3 3.3 %all-to-all-start.1 = ((bf16[1,8,2,128]{3,2,0,1:T(2,128)(2,1)}), bf16[1,8,2,128]{3,2,0,1:T(2,128)(2,1)S(1)}, u32[]{:S(2)}, u32[]{:S(2)}) async-start(bf16[1,8,2,128]{3,2,0,1:T(2,128)(2,1)} %fusion.162), calls=%async_computation.1 | async-start | bytes 8192 | tf_op jit(solution)/shard_map/all_to_all | solution.py:129
  141.7 6.5 %all-to-all-done.1 = bf16[1,8,2,128]{3,2,0,1:T(2,128)(2,1)S(1)} async-done(((bf16[1,8,2,128]{3,2,0,1:T(2,128)(2,1)}), bf16[1,8,2,128]{3,2,0,1:T(2,128)(2,1)S(1)}, u32[]{:S(2)}, u32[]{:S(2)}) %all-to-all-start.1) | async-done | bytes 4128 | tf_op jit(solution)/shard_map/all_to_all | solution.py:129
  148.2 0.8 fusion.160
  149.0 1.3 collective-permute-start.6
  150.6 1.5 collective-permute-done.6
  152.3 0.8 fusion.29
  153.1 7.4 %all-reduce.1 = (f32[4,256]{1,0:T(4,128)S(1)}, f32[4,256]{1,0:T(4,128)S(1)}) all-reduce(f32[4,256]{1,0:T(4,128)S(1)} %pad_maximum_fusion.8, f32[4,256]{1,0:T(4,128)S(1)} %pad_maximum_fusion.9), channel_id=1, replica_groups=mesh['seq'=4,'user'=8] {'seq'}, use_global_device_ids=true, to_apply=%region_22.0 | all-reduce | flops 2048 | bytes 16384 | tf_op jit(solution)/shard_map/psum | solution.py:116
  160.6 19.4 %all-reduce = (f32[4,256]{1,0:T(4,128)S(1)}, f32[4,256]{1,0:T(4,128)S(1)}) all-reduce(f32[4,256]{1,0:T(4,128)S(1)} %get-tuple-element.21, f32[4,256]{1,0:T(4,128)S(1)} %get-tuple-element.22), channel_id=1, replica_groups=mesh['seq'=4,'user'=8] {'user'}, use_global_device_ids=true, to_apply=%region_23.0 | all-reduce | flops 2048 | bytes 16384 | tf_op jit(solution)/shard_map/psum | solution.py:115
  180.0 0.6 broadcast_multiply_fusion.2
  180.6 0.6 broadcast_multiply_fusion.1
  181.2 1.0 fusion.28
  182.2 74.9 %all-reduce.7.cloned.1.call-done = f32[4,3,256,256]{3,2,1,0:T(8,128)} async-done(((f32[4,3,256,256]{3,2,1,0:T(8,128)}), f32[4,3,256,256]{3,2,1,0:T(8,128)}) %all-reduce.7.cloned.1.call-update) | async-done | bytes 3145744 | tf_op jit(solution)/shard_map/psum | solution.py:115
  257.1 3.8 %broadcast_multiply_fusion = f32[4,3,256,256]{3,2,1,0:T(8,128)} fusion(f32[4,3,256,256]{3,2,1,0:T(8,128)} %all-reduce.7.cloned.1.call-done), kind=kLoop, calls=%fused_computation.3 | loop fusion | flops 786432 | bytes 6291456 | tf_op jit(solution)/shard_map/mul | solution.py:135
  (89 shorter events, 9.5 us)
Async XLA Ops:
  7.2 124.6 %copy-start = (bf16[1,16,128]{2,1,0:T(8,128)(2,1)S(1)}, bf16[1,16,128]{2,1,0:T(8,128)(2,1)}, u32[]{:S(2)}) copy-start(bf16[1,16,128]{2,1,0:T(8,128)(2,1)} %param.13) | copy-start | bytes 12292
  7.2 11.2 %copy-start.3 = (bf16[1,512,256]{2,1,0:T(8,128)(2,1)S(1)}, bf16[1,512,256]{2,1,0:T(8,128)(2,1)}, u32[]{:S(2)}) copy-start(bf16[1,512,256]{2,1,0:T(8,128)(2,1)} %param.9) | copy-start | bytes 786436
  7.2 11.0 %copy-start.4 = (bf16[4,3,256,256]{3,2,1,0:T(8,128)(2,1)S(1)}, bf16[4,3,256,256]{3,2,1,0:T(8,128)(2,1)}, u32[]{:S(2)}) copy-start(bf16[4,3,256,256]{3,2,1,0:T(8,128)(2,1)} %param.10) | copy-start | bytes 4718596
  7.2 117.0 %all-reduce.5.cloned.1.call-start = ((), (), s32[]{:S(2)}) async-start(), calls=%async_computation.2 | async-start | bytes 6291456 | tf_op jit(solution)/shard_map/psum | solution.py:116
  11.7 6.7 %collective-permute-start = (bf16[1,2,256]{2,1,0:T(2,128)(2,1)S(1)}, bf16[1,2,256]{2,1,0:T(2,128)(2,1)S(1)}, u32[]{:S(2)}, u32[]{:S(2)}) collective-permute-start(bf16[1,2,256]{2,1,0:T(2,128)(2,1)S(1)} %slice.220), channel_id=1, source_target_pairs={{0,8},{8,16},{16,24},{1,9},{9,17},{17,25},{2,10},{10,18},{18,26},{... | collective-permute-start | bytes 3080 | tf_op jit(solution)/shard_map/ppermute | solution.py:15
  14.8 17.6 %collective-permute-start.3 = (bf16[1,16,256]{2,1,0:T(8,128)(2,1)S(1)}, bf16[1,16,256]{2,1,0:T(8,128)(2,1)S(1)}, u32[]{:S(2)}, u32[]{:S(2)}) collective-permute-start(bf16[1,16,256]{2,1,0:T(8,128)(2,1)S(1)} %slice.198), channel_id=1, source_target_pairs={{8,0},{16,8},{24,16},{9,1},{17,9},{25,17},{10,2},{18,10},{26,18},{... | collective-permute-start | bytes 24584 | tf_op jit(solution)/shard_map/ppermute | solution.py:15
  18.1 1.0 copy-start.2
  20.0 6.0 %collective-permute-start.1 = (bf16[1,4,256]{2,1,0:T(4,128)(2,1)S(1)}, bf16[1,4,256]{2,1,0:T(4,128)(2,1)S(1)}, u32[]{:S(2)}, u32[]{:S(2)}) collective-permute-start(bf16[1,4,256]{2,1,0:T(4,128)(2,1)S(1)} %slice.223), channel_id=1, source_target_pairs={{0,8},{8,16},{16,24},{1,9},{9,17},{17,25},{2,10},{10,18},{18,26},{... | collective-permute-start | bytes 6152 | tf_op jit(solution)/shard_map/ppermute | solution.py:15
  27.2 4.4 %collective-permute-start.2 = (bf16[1,8,256]{2,1,0:T(8,128)(2,1)S(1)}, bf16[1,8,256]{2,1,0:T(8,128)(2,1)S(1)}, u32[]{:S(2)}, u32[]{:S(2)}) collective-permute-start(bf16[1,8,256]{2,1,0:T(8,128)(2,1)S(1)} %slice.226), channel_id=1, source_target_pairs={{0,8},{8,16},{16,24},{1,9},{9,17},{17,25},{2,10},{10,18},{18,26},{... | collective-permute-start | bytes 12296 | tf_op jit(solution)/shard_map/ppermute | solution.py:15
  34.8 6.7 %collective-permute-start.4 = (bf16[1,8,256]{2,1,0:T(8,128)(2,1)S(1)}, bf16[1,8,256]{2,1,0:T(8,128)(2,1)S(1)}, u32[]{:S(2)}, u32[]{:S(2)}) collective-permute-start(bf16[1,8,256]{2,1,0:T(8,128)(2,1)S(1)} %slice.231), channel_id=1, source_target_pairs={{8,0},{16,8},{24,16},{9,1},{17,9},{25,17},{10,2},{18,10},{26,18},{... | collective-permute-start | bytes 12296 | tf_op jit(solution)/shard_map/ppermute | solution.py:15
  36.1 14.6 %collective-permute-start.7 = (bf16[1,16,256]{2,1,0:T(8,128)(2,1)S(1)}, bf16[1,16,256]{2,1,0:T(8,128)(2,1)S(1)}, u32[]{:S(2)}, u32[]{:S(2)}) collective-permute-start(bf16[1,16,256]{2,1,0:T(8,128)(2,1)S(1)} %slice.240), channel_id=1, source_target_pairs={{0,8},{8,16},{16,24},{1,9},{9,17},{17,25},{2,10},{10,18},{18,26},{... | collective-permute-start | bytes 24584 | tf_op jit(solution)/shard_map/ppermute | solution.py:15
  43.5 4.8 %collective-permute-start.5 = (bf16[1,4,256]{2,1,0:T(4,128)(2,1)S(1)}, bf16[1,4,256]{2,1,0:T(4,128)(2,1)S(1)}, u32[]{:S(2)}, u32[]{:S(2)}) collective-permute-start(bf16[1,4,256]{2,1,0:T(4,128)(2,1)S(1)} %slice.234), channel_id=1, source_target_pairs={{8,0},{16,8},{24,16},{9,1},{17,9},{25,17},{10,2},{18,10},{26,18},{... | collective-permute-start | bytes 6152 | tf_op jit(solution)/shard_map/ppermute | solution.py:15
  53.3 0.7 copy-start.5
  53.3 203.8 %all-reduce.7.cloned.1.call-start = ((), (), s32[]{:S(2)}) async-start(), calls=%async_computation.3 | async-start | bytes 6291456 | tf_op jit(solution)/shard_map/psum | solution.py:115
  124.2 0.7 copy-start.1
  126.2 12.1 %all-to-all-start = ((s32[1,8,2]{2,0,1:T(1,128)}), s32[1,8,2]{2,0,1:T(1,128)S(1)}, u32[]{:S(2)}, u32[]{:S(2)}) async-start(s32[1,8,2]{2,0,1:T(1,128)} %bitcast.75), calls=%async_computation | async-start | bytes 8192 | tf_op jit(solution)/shard_map/all_to_all | solution.py:130
  138.3 9.9 %all-to-all-start.1 = ((bf16[1,8,2,128]{3,2,0,1:T(2,128)(2,1)}), bf16[1,8,2,128]{3,2,0,1:T(2,128)(2,1)S(1)}, u32[]{:S(2)}, u32[]{:S(2)}) async-start(bf16[1,8,2,128]{3,2,0,1:T(2,128)(2,1)} %fusion.162), calls=%async_computation.1 | async-start | bytes 8192 | tf_op jit(solution)/shard_map/all_to_all | solution.py:129
  149.0 3.0 %collective-permute-start.6 = (bf16[1,2,256]{2,1,0:T(2,128)(2,1)S(1)}, bf16[1,2,256]{2,1,0:T(2,128)(2,1)S(1)}, u32[]{:S(2)}, u32[]{:S(2)}) collective-permute-start(bf16[1,2,256]{2,1,0:T(2,128)(2,1)S(1)} %slice.237), channel_id=1, source_target_pairs={{8,0},{16,8},{24,16},{9,1},{17,9},{25,17},{10,2},{18,10},{26,18},{... | collective-permute-start | bytes 3080 | tf_op jit(solution)/shard_map/ppermute | solution.py:15
Sparse Core Ops, SparseCore 0:
  53.5 70.7 all-reduce.4
  127.8 129.2 all-reduce.6
